TPU v7x, 512 devices: a whole 4x8x8 slice. The times are simulated.
512 devices in a mesh: leaf: 32 (over z, x), group: 16 (over y, core).
Axes of the slice: x: 4, y: 8, z: 8, core: 2. Of those that a mesh axis runs over, the one named last changes fastest.
Arguments:
- low_solved: float32 [262144, 256], P(('group', 'leaf')), may hold values from -4 to 4, as said below
- low_basis: float32 [262144, 256], P(('group', 'leaf')), may hold values from -0.001933495 to 0.001933495, as said below
- upper_solved: float32 [262144, 512], P(('group', 'leaf')), may hold values from -4 to 4, as said below
- upper_basis: float32 [262144, 256], P(('group', 'leaf')), may hold values from -0.001171875 to 0.001171875, as said below
Outputs:
- pair_solved: float32 [262144, 256], P(('group', 'leaf'))
- next_solved: float32 [262144, 256], P(('group', 'leaf'))
Inputs may be any that keep to these rules, and one draw needn't show every extreme that they name: `low_solved`: independent entries of mean zero. `low_basis`: independent entries of mean zero. `upper_solved`: independent entries of mean zero. `upper_basis`: independent entries of mean zero.
All inputs are finite; a program needn't handle non-finite values.
Results may differ from a plain program's by a relative error of at most 0.0003.
Values sent between devices are 32-bit elements; how exact they have to be, the bound alone decides.
A program may use at most 64 MiB of HBM per device.

v0:
```python
import jax
import jax.numpy as jnp
from jax import lax
from jax.sharding import PartitionSpec as P

ITERS = 4


def partner(x, axis, stride):
    return lax.ppermute(x, axis, [(i, i ^ 1 << stride) for i in range(lax.axis_size(axis))])


def product(left, right):
    return jnp.dot(left, right, precision=lax.Precision.HIGHEST, preferred_element_type=jnp.float32)


def transposed_product(left, right):
    return lax.dot_general(
        left,
        right,
        (((0,), (0,)), ((), ())),
        precision=lax.Precision.HIGHEST,
        preferred_element_type=jnp.float32,
    )


def jacobi(couple_first, rhs_first, couple_second, rhs_second):
    update_first = jnp.zeros(rhs_second.shape, jnp.float32)
    update_second = jnp.zeros(rhs_first.shape, jnp.float32)
    for sweep_index in range(ITERS):
        update_first, update_second = (
            rhs_second - product(couple_second, update_second),
            rhs_first - product(couple_first, update_first),
        )
    return (update_first, update_second)


def body(low_solved, low_basis, upper_solved, upper_basis):
    rank_width = low_solved.shape[1]
    leaves = lax.axis_size("leaf")
    half_index = lax.axis_index("leaf") // (leaves // 2)
    slot_mask = (jnp.arange(2) == half_index).astype(jnp.float32)
    joined = jnp.concatenate([low_solved, upper_solved], axis=1)
    local_terms = transposed_product(low_basis, joined)
    totals = lax.psum(slot_mask[:, None, None] * local_terms[None], "leaf")
    first_half = totals[0]
    second_half = totals[1]
    update_first, update_second = jacobi(
        first_half[:, :rank_width],
        first_half[:, rank_width:],
        second_half[:, :rank_width],
        second_half[:, rank_width:],
    )
    own_update = jnp.where(half_index == 0, update_first, update_second)
    middle = upper_solved - product(low_solved, own_update)
    group_total = lax.psum(transposed_product(upper_basis, middle), "leaf")
    pair_solved = middle[:, :rank_width]
    sibling = partner(group_total, "group", 0)
    parity = lax.axis_index("group") % 2
    first_group = jnp.where(parity == 0, group_total, sibling)
    second_group = jnp.where(parity == 0, sibling, group_total)
    pair_first, pair_second = jacobi(
        first_group[:, :rank_width],
        first_group[:, rank_width:],
        second_group[:, :rank_width],
        second_group[:, rank_width:],
    )
    pair_update = jnp.where(parity == 0, pair_first, pair_second)
    next_solved = middle[:, rank_width:] - product(pair_solved, pair_update)
    return (pair_solved, next_solved)


def solution(mesh):
    return jax.shard_map(
        body,
        mesh=mesh,
        in_specs=(
            P(("group", "leaf"), None),
            P(("group", "leaf"), None),
            P(("group", "leaf"), None),
            P(("group", "leaf"), None),
        ),
        out_specs=(P(("group", "leaf"), None), P(("group", "leaf"), None)),
        check_vma=False,
    )
```

profile of v0, /device:TPU:1, one launch (start us, length us, event | category | flops | bytes accessed | tf_op | source)
XLA Modules:
  0.0 367.2 jit_solution(1575446684602732130)
XLA Ops:
  7.3 1.0 copy-done
  8.2 4.0 %fusion.5 = f32[256,768]{0,1:T(8,128)S(1)} fusion(f32[512,256]{1,0:T(8,128)S(1)} %copy-done, f32[512,512]{1,0:T(8,128)} %param.6, f32[512,256]{1,0:T(8,128)} %param.4), kind=kOutput, calls=%fused_computation.6 | convolution fusion | flops 1208352768 | bytes 2883584 | tf_op jit(solution)/shard_map/dot_general | solution.py:18
  12.2 0.3 copy.6
  12.5 1.3 broadcast_multiply_fusion
  13.9 0.1 copy-done.1
  14.0 0.3 copy.7
  14.3 164.7 %all-reduce.3.cloned.1.call-done = f32[2,256,768]{2,1,0:T(8,128)} async-done(((f32[2,256,768]{2,1,0:T(8,128)}), f32[2,256,768]{2,1,0:T(8,128)}) %all-reduce.3.cloned.1.call-update) | async-done | bytes 1572880 | tf_op jit(solution)/shard_map/psum | solution.py:45
  179.0 1.5 slice_bitcast_fusion.1
  180.5 0.6 convolution_subtract_fusion.4
  181.0 0.6 convolution_subtract_fusion.8
  181.6 0.6 convolution_subtract_fusion.3
  182.2 0.6 convolution_subtract_fusion.2
  182.9 0.6 convolution_subtract_fusion.7
  183.5 0.6 convolution_subtract_fusion.6
  184.1 0.6 convolution_subtract_fusion.5
  184.8 0.6 fusion.8
  185.4 1.9 fusion.4
  187.3 1.8 convolution_bitcast_fusion.1
  189.1 157.5 %all-reduce.5.cloned.1.call-done = f32[256,512]{0,1:T(8,128)} async-done(((f32[256,512]{0,1:T(8,128)}), f32[256,512]{0,1:T(8,128)}) %all-reduce.5.cloned.1.call-update) | async-done | bytes 524304 | tf_op jit(solution)/shard_map/psum | solution.py:56
  346.6 7.2 %collective-permute-start = (f32[256,512]{0,1:T(8,128)}, f32[256,512]{0,1:T(8,128)S(1)}, u32[]{:S(2)}, u32[]{:S(2)}) collective-permute-start(f32[256,512]{0,1:T(8,128)} %all-reduce.5.cloned.1.call-done), channel_id=1, source_target_pairs={{0,1},{1,0},{2,3},{3,2},{4,5},{5,4},{6,7},{7,6},{8,9},{9,8},{10,11... | collective-permute-start | bytes 1572872 | tf_op jit(solution)/shard_map/ppermute | solution.py:10
  353.9 1.0 copy.9
  354.9 0.5 collective-permute-done
  355.5 0.4 convolution_subtract_fusion.16
  355.9 0.4 convolution_subtract_fusion.12
  356.3 0.4 convolution_subtract_fusion.15
  356.7 0.4 convolution_subtract_fusion.14
  357.1 0.4 convolution_subtract_fusion.11
  357.5 0.4 convolution_subtract_fusion.10
  357.9 0.4 convolution_subtract_fusion.9
  358.3 0.4 fusion.9
  358.7 0.6 convolution_subtract_fusion
  359.3 1.0 copy.10
  (15 shorter events, 0.3 us)
Async XLA Ops:
  7.2 1.0 copy-start
  7.2 171.8 %all-reduce.3.cloned.1.call-start = ((), (), s32[]{:S(2)}) async-start(), calls=%async_computation | async-start | bytes 3145728 | tf_op jit(solution)/shard_map/psum | solution.py:45
  12.5 1.5 copy-start.1
  13.8 332.8 %all-reduce.5.cloned.1.call-start = ((), (), s32[]{:S(2)}) async-start(), calls=%async_computation.1 | async-start | bytes 1048576 | tf_op jit(solution)/shard_map/psum | solution.py:56
  184.1 1.3 copy-start.2
  185.4 1.9 copy-start.4
  346.6 8.8 %copy-start.3 = (f32[256,512]{0,1:T(8,128)S(1)}, f32[256,512]{0,1:T(8,128)}, u32[]{:S(2)}) copy-start(f32[256,512]{0,1:T(8,128)} %all-reduce.5.cloned.1.call-done) | copy-start | bytes 1572868
  346.6 8.8 %collective-permute-start = (f32[256,512]{0,1:T(8,128)}, f32[256,512]{0,1:T(8,128)S(1)}, u32[]{:S(2)}, u32[]{:S(2)}) collective-permute-start(f32[256,512]{0,1:T(8,128)} %all-reduce.5.cloned.1.call-done), channel_id=1, source_target_pairs={{0,1},{1,0},{2,3},{3,2},{4,5},{5,4},{6,7},{7,6},{8,9},{9,8},{10,11... | collective-permute-start | bytes 1572872 | tf_op jit(solution)/shard_map/ppermute | solution.py:10
Sparse Core Ops, SparseCore 0:
  13.9 165.0 all-reduce.2
  189.2 157.3 all-reduce.4
where the time goes:
time: 367 us
  waiting for transfers between devices  323 us (88%)
  matrix products  16.3 us (4%)
  between operations  14.3 us (4%)
  starting transfers between devices  7.31 us (2%)
  local copies, waits for them, and re-layouts  5.18 us (1%)
    psum x1, waiting for transfers between devices, body(): totals = lax.psum(slot_mask[:, None, None] * local_terms[None], 'leaf')  165 us
    psum x1, waiting for transfers between devices, body(): group_total = lax.psum(transposed_product(upper_basis, middle), 'leaf')  157 us
    dot_general x18, matrix products, product(): jnp.dot(left, right, precision=lax.Precision.HIGHEST, preferred_element_t...  10.5 us
  transfers between devices with their start and end apart: 3, of which 3 were waited for; matrix products, arithmetic and copies ran while one was open for 0% of the time, Pallas kernels for 0%

commit v1 on v0

--- a/solution.py
+++ b/solution.py
@@ -53,7 +53,11 @@
     )
     own_update = jnp.where(half_index == 0, update_first, update_second)
     middle = upper_solved - product(low_solved, own_update)
-    group_total = lax.psum(transposed_product(upper_basis, middle), "leaf")
+
+    def finish_the_slots(xs):
+        return lax.all_gather(xs, "leaf").sum(axis=0)
+
+    group_total = finish_the_slots(transposed_product(upper_basis, middle))
     pair_solved = middle[:, :rank_width]
     sibling = partner(group_total, "group", 0)
     parity = lax.axis_index("group") % 2

time: 367 us -> 386 us (1.052)
  local copies, waits for them, and re-layouts: 5.18 us -> 21 us
  other arithmetic: 1.4 us -> 10.1 us
  waiting for transfers between devices: 323 us -> 318 us
    psum x1 -> x0, waiting for transfers between devices: 157 us -> none  [body(): group_total = lax.psum(transposed_product(upper_basis, middle), 'leaf')]
    all_gather x0 -> x1, waiting for transfers between devices: none -> 153 us  [finish_the_slots(): return lax.all_gather(xs, 'leaf').sum(axis=0)]
    unnamed x13 -> x12, local copies, waits for them, and re-layouts: 3.41 us -> 19.2 us
    reduce_sum x0 -> x1, other arithmetic: none -> 8.68 us  [finish_the_slots(): return lax.all_gather(xs, 'leaf').sum(axis=0)]
where the time goes in v1:
time: 386 us
  waiting for transfers between devices  318 us (82%)
  local copies, waits for them, and re-layouts  21 us (5%)
  matrix products  16.3 us (4%)
  between operations  14.3 us (4%)
  other arithmetic  10.1 us (3%)
  starting transfers between devices  5.78 us (1%)
    psum x1, waiting for transfers between devices, body(): totals = lax.psum(slot_mask[:, None, None] * local_terms[None], 'leaf')  165 us
    all_gather x1, waiting for transfers between devices, finish_the_slots(): return lax.all_gather(xs, 'leaf').sum(axis=0)  153 us
    unnamed x12, local copies, waits for them, and re-layouts  19.2 us
    dot_general x18, matrix products, product(): jnp.dot(left, right, precision=lax.Precision.HIGHEST, preferred_element_t...  10.5 us
    reduce_sum x1, other arithmetic, finish_the_slots(): return lax.all_gather(xs, 'leaf').sum(axis=0)  8.68 us
  transfers between devices with their start and end apart: 3, of which 3 were waited for; matrix products, arithmetic and copies ran while one was open for 0% of the time, Pallas kernels for 0%

profile of v1, /device:TPU:1, one launch (start us, length us, event | category | flops | bytes accessed | tf_op | source)
XLA Modules:
  0.0 385.8 jit_solution(11633000419148634014)
XLA Ops:
  7.3 1.0 copy-done
  8.2 4.0 %fusion.5 = f32[256,768]{0,1:T(8,128)S(1)} fusion(f32[512,256]{1,0:T(8,128)S(1)} %copy-done, f32[512,512]{1,0:T(8,128)} %param.6, f32[512,256]{1,0:T(8,128)} %param.4), kind=kOutput, calls=%fused_computation.7 | convolution fusion | flops 1208352768 | bytes 2883584 | tf_op jit(solution)/shard_map/dot_general | solution.py:18
  12.5 1.3 broadcast_multiply_fusion
  14.0 0.3 copy.12
  14.3 164.7 %all-reduce.2.cloned.1.call-done = f32[2,256,768]{2,1,0:T(8,128)} async-done(((f32[2,256,768]{2,1,0:T(8,128)}), f32[2,256,768]{2,1,0:T(8,128)}) %all-reduce.2.cloned.1.call-update) | async-done | bytes 1572880 | tf_op jit(solution)/shard_map/psum | solution.py:45
  179.0 1.5 slice_bitcast_fusion.1
  180.5 0.6 convolution_subtract_fusion.4
  181.1 0.6 convolution_subtract_fusion.8
  181.6 0.6 convolution_subtract_fusion.3
  182.3 0.6 convolution_subtract_fusion.2
  182.9 0.6 convolution_subtract_fusion.7
  183.5 0.6 convolution_subtract_fusion.6
  184.2 0.6 convolution_subtract_fusion.5
  184.8 0.6 fusion.8
  185.4 1.9 fusion.4
  187.3 1.8 convolution_bitcast_fusion.1
  189.1 153.2 %all-gather.3.cloned.1.call-done = f32[8192,512]{0,1:T(8,128)} async-done(((f32[256,512]{0,1:T(8,128)}), f32[8192,512]{0,1:T(8,128)}) %all-gather.3.cloned.1.call-update) | async-done | bytes 16777232 | tf_op jit(solution)/shard_map/all_gather | solution.py:58
  342.3 15.8 %copy.17 = f32[64,8,32,256]{3,2,1,0:T(8,128)} copy(f32[64,8,32,256]{3,1,2,0:T(8,128)} %bitcast.35) | data formatting | bytes 33554432
  358.1 8.7 %bitcast_reduce_fusion = f32[256,512]{0,1:T(8,128)S(1)} fusion(f32[64,8,32,256]{3,2,1,0:T(8,128)} %copy.17), kind=kLoop, calls=%fused_computation | loop fusion | flops 4063232 | bytes 17301504 | tf_op jit(solution)/shard_map/reduce_sum | solution.py:58
  366.8 5.7 %collective-permute-start = (f32[256,512]{0,1:T(8,128)S(1)}, f32[256,512]{0,1:T(8,128)S(1)}, u32[]{:S(2)}, u32[]{:S(2)}) collective-permute-start(f32[256,512]{0,1:T(8,128)S(1)} %bitcast_reduce_fusion), channel_id=1, source_target_pairs={{0,1},{1,0},{2,3},{3,2},{4,5},{5,4},{6,7},{7,6},{8,9},{9,8},{10,11... | collective-permute-start | bytes 1572872 | tf_op jit(solution)/shard_map/ppermute | solution.py:10
  372.6 1.0 copy.14
  373.6 0.5 collective-permute-done
  374.1 0.4 convolution_subtract_fusion.16
  374.5 0.4 convolution_subtract_fusion.12
  374.9 0.4 convolution_subtract_fusion.15
  375.3 0.4 convolution_subtract_fusion.14
  375.7 0.4 convolution_subtract_fusion.11
  376.1 0.4 convolution_subtract_fusion.10
  376.5 0.4 convolution_subtract_fusion.9
  376.9 0.4 fusion.9
  377.3 0.6 convolution_subtract_fusion
  378.0 1.0 copy.15
  (15 shorter events, 0.6 us)
Async XLA Ops:
  7.2 1.0 copy-start
  7.2 171.8 %all-reduce.2.cloned.1.call-start = ((), (), s32[]{:S(2)}) async-start(), calls=%async_computation | async-start | bytes 3145728 | tf_op jit(solution)/shard_map/psum | solution.py:45
  12.5 1.5 copy-start.1
  13.8 328.5 %all-gather.3.cloned.1.call-start = ((), (), s32[]{:S(2)}) async-start(), calls=%async_computation.1 | async-start | bytes 17301504 | tf_op jit(solution)/shard_map/all_gather | solution.py:58
  184.1 1.3 copy-start.2
  185.4 1.9 copy-start.3
  366.8 7.2 %collective-permute-start = (f32[256,512]{0,1:T(8,128)S(1)}, f32[256,512]{0,1:T(8,128)S(1)}, u32[]{:S(2)}, u32[]{:S(2)}) collective-permute-start(f32[256,512]{0,1:T(8,128)S(1)} %bitcast_reduce_fusion), channel_id=1, source_target_pairs={{0,1},{1,0},{2,3},{3,2},{4,5},{5,4},{6,7},{7,6},{8,9},{9,8},{10,11... | collective-permute-start | bytes 1572872 | tf_op jit(solution)/shard_map/ppermute | solution.py:10
Sparse Core Ops, SparseCore 0:
  13.9 165.0 all-reduce.1
  189.2 153.0 all-gather.2
